TPU v7x, 32 devices: a whole 2x2x4 slice. The times are simulated.
32 devices in a mesh: dp: 4 (over z), mp: 8 (over y, x, core).
Axes of the slice: x: 2, y: 2, z: 4, core: 2. Of those that a mesh axis runs over, the one named last changes fastest.
Arguments:
- behaviors: bfloat16 [32, 2048, 1024], P('dp', 'mp'), may hold values from -8 to 8
- candidates: bfloat16 [32, 2048, 128], P('dp', 'mp'), may hold values from -12 to 12
- lengths: int32 [32], P('dp'), may hold values from 128 to 1024
- bilinear: bfloat16 [2048, 2048], P('mp'), may hold values from -1 to 2
- norm_gain: float32 [2048], replicated, may hold values from 0.1 to 1.9
- w_gate: bfloat16 [2048, 8192], P('dp', 'mp'), may hold values from -0.125 to 0.125
- w_up: bfloat16 [2048, 8192], P('dp', 'mp'), may hold values from -0.125 to 0.125
- w_down: bfloat16 [8192, 2048], P('mp', 'dp'), may hold values from -0.0625 to 0.0625
Outputs:
- interest: bfloat16 [32, 2048, 128], P('dp', 'mp')
All inputs are finite; a program needn't handle non-finite values.
Results may differ from a plain program's by a relative error of at most 0.015.
Values may be sent and summed in bfloat16 or wider, within the bound.
No kernel may reach another device: no remote copies, remote signals or barrier semaphores. Data moves between devices by JAX's collectives and lax.ppermute only.
A program may use at most 64 MiB of HBM per device.

v0:
```python
import math
import jax
import jax.numpy as jnp
from jax import lax
from jax.sharding import PartitionSpec as P


def attention_weights(scores, live):
    masked = jnp.where(live, scores, -1e30)
    highest = jnp.max(masked, axis=-1, keepdims=True)
    expons = jnp.where(live, jnp.exp(masked - highest), 0.0)
    return (expons / jnp.sum(expons, axis=-1, keepdims=True)).astype(jnp.bfloat16)


def shards(behaviors, candidates, lengths, bilinear, norm_gain, w_gate, w_up, w_down):
    user_count, width_part, cand_count = candidates.shape
    feature_width = bilinear.shape[1]
    behavior_count = behaviors.shape[2]
    query_part = jnp.einsum(
        "ek,ukc->uec",
        bilinear,
        lax.all_gather(candidates, "mp", axis=1, tiled=True),
        preferred_element_type=jnp.float32,
    )
    query = query_part.astype(jnp.bfloat16)
    partial_value = jnp.einsum("ukc,ukl->ucl", query, behaviors, preferred_element_type=jnp.float32)
    scale = 1.0 / math.sqrt(feature_width)
    live = (
        lax.broadcasted_iota(jnp.int32, (user_count, 1, behavior_count), 2) < lengths[:, None, None]
    )
    share = lax.psum_scatter(partial_value, "mp", scatter_dimension=1, tiled=True)
    probs_share = attention_weights(share * scale, live)
    probs = lax.all_gather(probs_share, "mp", axis=1, tiled=True)
    pooled = jnp.einsum(
        "ucl,ukl->ukc", probs, behaviors, preferred_element_type=jnp.float32
    ).astype(jnp.bfloat16)
    whole = lax.all_gather(pooled, "mp", axis=1, tiled=True)
    values = whole.astype(jnp.float32)
    square_mean = jnp.mean(values * values, axis=1, keepdims=True)
    normed = (values * lax.rsqrt(square_mean + 1e-06) * norm_gain[None, :, None]).astype(
        jnp.bfloat16
    )
    gate = jnp.einsum(
        "ukc,kf->ucf",
        normed,
        lax.all_gather(w_gate, "dp", axis=0, tiled=True),
        preferred_element_type=jnp.float32,
    )
    upward = jnp.einsum(
        "ukc,kf->ucf",
        normed,
        lax.all_gather(w_up, "dp", axis=0, tiled=True),
        preferred_element_type=jnp.float32,
    )
    hidden = (jax.nn.silu(gate) * upward).astype(jnp.bfloat16)
    down_full = lax.all_gather(w_down, "dp", axis=1, tiled=True)
    result = lax.psum_scatter(
        jnp.einsum("ucf,fk->kuc", hidden, down_full, preferred_element_type=jnp.float32).astype(
            jnp.bfloat16
        ),
        "mp",
        scatter_dimension=0,
        tiled=True,
    ).astype(jnp.float32)
    return jnp.transpose(result, (1, 0, 2)).astype(jnp.bfloat16)


def solution(mesh):
    return jax.shard_map(
        shards,
        mesh=mesh,
        in_specs=(
            P("dp", "mp", None),
            P("dp", "mp", None),
            P("dp"),
            P("mp", None),
            P(),
            P("dp", "mp"),
            P("dp", "mp"),
            P("mp", "dp"),
        ),
        out_specs=P("dp", "mp", None),
        check_vma=False,
    )
```

profile of v0, /device:TPU:0, one launch (start us, length us, event | category | flops | bytes accessed | tf_op | source)
XLA Modules:
  0.0 498.7 jit_solution(1023455317639719504)
XLA Ops:
  6.5 0.7 all-gather.7.cloned.1.call-update
  7.3 0.0 reduce-scatter.3.cloned.1.call-start
  7.3 41.3 %all-gather.7.cloned.1.call-done = bf16[8,2048,128]{2,1,0:T(8,128)(2,1)} async-done(((bf16[8,256,128]{2,1,0:T(8,128)(2,1)}), bf16[8,2048,128]{2,1,0:T(8,128)(2,1)}) %all-gather.7.cloned.1.call-update) | async-done | bytes 4194320 | tf_op jit(solution)/shard_map/all_gather | solution.py:22
  48.6 8.2 %fusion.24 = f32[8,128,1024]{2,1,0:T(8,128)} fusion(bf16[8,256,1024]{2,1,0:T(8,128)(2,1)} %param.8, bf16[8,2048,128]{2,1,0:T(8,128)(2,1)} %all-gather.7.cloned.1.call-done, bf16[256,2048]{1,0:T(8,128)(2,1)S(1)} %copy-done), kind=kOutput, calls=%fused_computation.18 | convolution fusion | flops 1610874880 | bytes 13631488 | tf_op jit(solution)/shard_map/ukc,ukl->ucl/dot_general | solution.py:26
  56.7 0.0 reduce-scatter.3.cloned.1.call-update
  56.8 0.0 all-gather.9.cloned.1.call-start
  56.8 0.6 copy-done.1
  57.4 0.1 iota_compare_fusion
  57.5 50.5 %reduce-scatter.3.cloned.1.call-done = f32[8,16,1024]{2,1,0:T(8,128)} async-done(((f32[8,128,1024]{2,1,0:T(8,128)}), f32[8,16,1024]{2,1,0:T(8,128)}) %reduce-scatter.3.cloned.1.call-update) | async-done | bytes 524304 | tf_op jit(solution)/shard_map/reduce_scatter | solution.py:31
  108.0 1.7 fusion.37
  109.7 0.8 divide_convert_fusion
  110.5 0.0 all-gather.9.cloned.1.call-update
  110.6 0.0 all-gather.11.cloned.1.call-start
  110.6 27.9 %all-gather.9.cloned.1.call-done = bf16[8,128,1024]{2,1,0:T(8,128)(2,1)} async-done(((bf16[8,16,1024]{2,1,0:T(8,128)(2,1)}), bf16[8,128,1024]{2,1,0:T(8,128)(2,1)}) %all-gather.9.cloned.1.call-update) | async-done | bytes 2097168 | tf_op jit(solution)/shard_map/all_gather | solution.py:33
  138.5 5.2 %fusion.27 = bf16[8,256,128]{1,2,0:T(8,128)(2,1)} fusion(bf16[8,128,1024]{2,1,0:T(8,128)(2,1)} %all-gather.9.cloned.1.call-done, bf16[8,256,1024]{2,1,0:T(8,128)(2,1)} %param.8), kind=kOutput, calls=%fused_computation.21 | convolution fusion | flops 537133056 | bytes 6815744 | tf_op jit(solution)/shard_map/ucl,ukl->ukc/dot_general | solution.py:34
  143.7 0.0 all-gather.13.cloned.1.call-start
  143.7 0.5 all-gather.13.cloned.1.call-update
  144.3 0.0 all-gather.15.cloned.1.call-start
  144.3 0.5 all-gather.15.cloned.1.call-update
  144.8 0.0 all-gather.17.cloned.1.call-start
  144.9 0.7 all-gather.17.cloned.1.call-update
  145.6 0.2 reduce-scatter.5.cloned.1.call-start
  145.8 35.4 %all-gather.11.cloned.1.call-done = bf16[8,2048,128]{1,2,0:T(8,128)(2,1)} async-done(((bf16[8,256,128]{1,2,0:T(8,128)(2,1)}), bf16[8,2048,128]{1,2,0:T(8,128)(2,1)}) %all-gather.11.cloned.1.call-update) | async-done | bytes 4194320 | tf_op jit(solution)/shard_map/all_gather | solution.py:37
  181.2 3.1 fusion.1
  184.3 79.1 %all-gather.13.cloned.1.call-done = bf16[2048,1024]{1,0:T(8,128)(2,1)} async-done(((bf16[512,1024]{1,0:T(8,128)(2,1)}), bf16[2048,1024]{1,0:T(8,128)(2,1)}) %all-gather.13.cloned.1.call-update) | async-done | bytes 4194320 | tf_op jit(solution)/shard_map/all_gather | solution.py:46
  263.4 9.9 %fusion.8 = f32[8,128,1024]{2,1,0:T(8,128)} fusion(bf16[2048,1024]{1,0:T(8,128)(2,1)} %all-gather.13.cloned.1.call-done, bf16[8,2048,128]{1,2,0:T(8,128)(2,1)} %all-gather.11.cloned.1.call-done, f32[2048]{0:T(1024)S(1)} %copy-done.2, f32[8,128]{1,0:T(8,128)S(1)} %add_rsqrt_fusion), kind=kOutput, calls=%fused_computation.10 | convolution fusion | flops 4303355904 | bytes 12595200 | tf_op jit(solution)/shard_map/ukc,kf->ucf/dot_general | solution.py:43
  273.3 70.7 %all-gather.15.cloned.1.call-done = bf16[2048,1024]{1,0:T(8,128)(2,1)} async-done(((bf16[512,1024]{1,0:T(8,128)(2,1)}), bf16[2048,1024]{1,0:T(8,128)(2,1)}) %all-gather.15.cloned.1.call-update) | async-done | bytes 4194320 | tf_op jit(solution)/shard_map/all_gather | solution.py:52
  344.0 80.8 %all-gather.17.cloned.1.call-done = bf16[1024,2048]{1,0:T(8,128)(2,1)} async-done(((bf16[1024,512]{1,0:T(8,128)(2,1)}), bf16[1024,2048]{1,0:T(8,128)(2,1)}) %all-gather.17.cloned.1.call-update) | async-done | bytes 4194320 | tf_op jit(solution)/shard_map/all_gather | solution.py:56
  424.9 15.2 %convert_bitcast_fusion = bf16[2048,8,128]{0,2,1:T(8,128)(2,1)} fusion(bf16[1024,2048]{1,0:T(8,128)(2,1)} %all-gather.17.cloned.1.call-done, f32[8,128,1024]{2,1,0:T(8,128)} %fusion.8, bf16[2048,1024]{1,0:T(8,128)(2,1)} %all-gather.15.cloned.1.call-done, bf16[8,2048,128]{1,2,0:T(8,128)(2,1)} %all-gather.11.cloned.1.call-done, f32[2048]{0:T(1024)S(1)} %copy-done.2, ...), kind=kOutput, calls=%fused_computation.12 | convolution fusion | flops 8606711808 | bytes 20983808 | tf_op jit(solution)/shard_map/ucf,fk->kuc/dot_general | solution.py:58
  440.1 0.0 reduce-scatter.5.cloned.1.call-update
  440.1 49.7 %reduce-scatter.5.cloned.1.call-done = bf16[256,8,128]{0,2,1:T(8,128)(2,1)} async-done(((bf16[2048,8,128]{0,2,1:T(8,128)(2,1)}), bf16[256,8,128]{0,2,1:T(8,128)(2,1)}) %reduce-scatter.5.cloned.1.call-update) | async-done | bytes 524304 | tf_op jit(solution)/shard_map/reduce_scatter | solution.py:57
  489.8 2.0 copy.9
  (8 shorter events, 0.0 us)
Async XLA Ops:
  6.5 42.0 %copy-start = (bf16[256,2048]{1,0:T(8,128)(2,1)S(1)}, bf16[256,2048]{1,0:T(8,128)(2,1)}, u32[]{:S(2)}) copy-start(bf16[256,2048]{1,0:T(8,128)(2,1)} %param.11) | copy-start | bytes 3145732
  6.5 42.0 %all-gather.7.cloned.1.call-start = ((), (), s32[]{:S(2)}) async-start(), calls=%async_computation.2 | async-start | bytes 4718592 | tf_op jit(solution)/shard_map/all_gather | solution.py:22
  7.3 100.8 %reduce-scatter.3.cloned.1.call-start = ((), (), s32[]{:S(2)}) async-start(), calls=%async_computation.3 | async-start | bytes 4718592 | tf_op jit(solution)/shard_map/reduce_scatter | solution.py:31
  56.7 0.7 copy-start.1
  56.8 81.7 %all-gather.9.cloned.1.call-start = ((), (), s32[]{:S(2)}) async-start(), calls=%async_computation.4 | async-start | bytes 2359296 | tf_op jit(solution)/shard_map/all_gather | solution.py:33
  110.6 70.6 %all-gather.11.cloned.1.call-start = ((), (), s32[]{:S(2)}) async-start(), calls=%async_computation.5 | async-start | bytes 4718592 | tf_op jit(solution)/shard_map/all_gather | solution.py:37
  143.7 119.7 %copy-start.2 = (f32[2048]{0:T(1024)S(1)}, f32[2048]{0:T(1024)}, u32[]{:S(2)}) copy-start(f32[2048]{0:T(1024)} %param.12) | copy-start | bytes 24580
  143.7 119.7 %all-gather.13.cloned.1.call-start = ((), (), s32[]{:S(2)}) async-start(), calls=%async_computation.6 | async-start | bytes 5242880 | tf_op jit(solution)/shard_map/all_gather | solution.py:46
  144.3 199.8 %all-gather.15.cloned.1.call-start = ((), (), s32[]{:S(2)}) async-start(), calls=%async_computation.7 | async-start | bytes 5242880 | tf_op jit(solution)/shard_map/all_gather | solution.py:52
  144.8 280.0 %all-gather.17.cloned.1.call-start = ((), (), s32[]{:S(2)}) async-start(), calls=%async_computation.8 | async-start | bytes 5242880 | tf_op jit(solution)/shard_map/all_gather | solution.py:56
  145.6 344.2 %reduce-scatter.5.cloned.1.call-start = ((), (), s32[]{:S(2)}) async-start(), calls=%async_computation.9 | async-start | bytes 4718592 | tf_op jit(solution)/shard_map/reduce_scatter | solution.py:57
Sparse Core Ops, SparseCore 0:
  9.2 39.2 all-gather.6
  56.9 51.0 reduce-scatter.2
  110.7 27.7 all-gather.8
  143.8 37.3 all-gather.10
  182.6 80.7 all-gather.12
  264.8 79.2 all-gather.14
  345.6 79.2 all-gather.16
  440.2 49.5 reduce-scatter.4
where the time goes:
time: 499 us
  waiting for transfers between devices  438 us (88%)
  matrix products  38.4 us (8%)
  between operations  13.5 us (3%)
  other arithmetic  5.68 us (1%)
    all_gather x1, waiting for transfers between devices, shards(): down_full = lax.all_gather(w_down, 'dp', axis=1, tiled=True)  80.8 us
    all_gather x1, waiting for transfers between devices, shards(): lax.all_gather(w_gate, 'dp', axis=0, tiled=True)  79.1 us
    all_gather x1, waiting for transfers between devices, shards(): lax.all_gather(w_up, 'dp', axis=0, tiled=True)  70.7 us
    reduce_scatter x1, waiting for transfers between devices, shards(): lax.psum_scatter(partial_value, 'mp', scatter_dimension=1, tiled=True)  50.5 us
    reduce_scatter x1, waiting for transfers between devices, shards(): lax.psum_scatter(jnp.einsum('ucf,fk->kuc', hidden, down_full, preferred_e...  49.7 us
    all_gather x1, waiting for transfers between devices, shards(): lax.all_gather(candidates, 'mp', axis=1, tiled=True)  41.3 us
    all_gather x1, waiting for transfers between devices, shards(): whole = lax.all_gather(pooled, 'mp', axis=1, tiled=True)  35.4 us
    all_gather x1, waiting for transfers between devices, shards(): probs = lax.all_gather(probs_share, 'mp', axis=1, tiled=True)  27.9 us
  transfers between devices with their start and end apart: 8, of which 8 were waited for; matrix products, arithmetic and copies ran while one was open for 3% of the time, Pallas kernels for 0%

commit v1 on v0

--- a/solution.py
+++ b/solution.py
@@ -3,6 +3,7 @@
 import jax.numpy as jnp
 from jax import lax
 from jax.sharding import PartitionSpec as P
+from jax.lax import axis_index, axis_size, ppermute
 
 
 def attention_weights(scores, live):
@@ -16,12 +17,25 @@
     user_count, width_part, cand_count = candidates.shape
     feature_width = bilinear.shape[1]
     behavior_count = behaviors.shape[2]
+    after = axis_size("mp")
+    e_next, e_now = (after, axis_index("mp"))
+    sheets = [(j, (j - 1) % e_next) for j in range(e_next)]
+    t1 = candidates.shape[1]
+    w2 = candidates
     query_part = jnp.einsum(
         "ek,ukc->uec",
-        bilinear,
-        lax.all_gather(candidates, "mp", axis=1, tiled=True),
+        lax.dynamic_slice_in_dim(bilinear, e_now * t1, w2.shape[1], axis=1),
+        w2,
         preferred_element_type=jnp.float32,
     )
+    for h in range(1, e_next):
+        w2 = ppermute(w2, axis_name="mp", perm=sheets)
+        query_part = query_part + jnp.einsum(
+            "ek,ukc->uec",
+            lax.dynamic_slice_in_dim(bilinear, (e_now + h) % e_next * t1, w2.shape[1], axis=1),
+            w2,
+            preferred_element_type=jnp.float32,
+        )
     query = query_part.astype(jnp.bfloat16)
     partial_value = jnp.einsum("ukc,ukl->ucl", query, behaviors, preferred_element_type=jnp.float32)
     scale = 1.0 / math.sqrt(feature_width)

time: 499 us -> 523 us (1.048)
  starting transfers between devices: 0.46 us -> 20.5 us
    ppermute x0 -> x7, waiting for transfers between devices: none -> 43.7 us  [shards(): w2 = ppermute(w2, axis_name='mp', perm=sheets)]
    all_gather x1 -> x0, waiting for transfers between devices: 41.3 us -> none  [shards(): lax.all_gather(candidates, 'mp', axis=1, tiled=True)]
    ppermute x0 -> x7, starting transfers between devices: none -> 20.1 us  [shards(): w2 = ppermute(w2, axis_name='mp', perm=sheets)]
  transfers between devices with their start and end apart: 8 -> 14, of which waited for: 8 -> 14; matrix products, arithmetic and copies ran while one was open for 3% -> 3% of each run, Pallas kernels for 0% -> 0%
where the time goes in v1:
time: 523 us; the launch traced here: 522 us
  waiting for transfers between devices  441 us (84%)
  matrix products  39 us (7%)
  starting transfers between devices  20.5 us (4%)
  between operations  13.6 us (3%)
  other arithmetic  5.65 us (1%)
    all_gather x1, waiting for transfers between devices, shards(): down_full = lax.all_gather(w_down, 'dp', axis=1, tiled=True)  80.7 us
    all_gather x1, waiting for transfers between devices, shards(): lax.all_gather(w_gate, 'dp', axis=0, tiled=True)  79.1 us
    all_gather x1, waiting for transfers between devices, shards(): lax.all_gather(w_up, 'dp', axis=0, tiled=True)  70.7 us
    reduce_scatter x1, waiting for transfers between devices, shards(): lax.psum_scatter(partial_value, 'mp', scatter_dimension=1, tiled=True)  52.2 us
    reduce_scatter x1, waiting for transfers between devices, shards(): lax.psum_scatter(jnp.einsum('ucf,fk->kuc', hidden, down_full, preferred_e...  49.7 us
    ppermute x7, waiting for transfers between devices, shards(): w2 = ppermute(w2, axis_name='mp', perm=sheets)  43.7 us
    all_gather x1, waiting for transfers between devices, shards(): whole = lax.all_gather(pooled, 'mp', axis=1, tiled=True)  35.5 us
    all_gather x1, waiting for transfers between devices, shards(): probs = lax.all_gather(probs_share, 'mp', axis=1, tiled=True)  27.9 us
  transfers between devices with their start and end apart: 14, of which 14 were waited for; matrix products, arithmetic and copies ran while one was open for 3% of the time, Pallas kernels for 0%

profile of v1, /device:TPU:0, one launch (start us, length us, event | category | flops | bytes accessed | tf_op | source)
XLA Modules:
  0.0 522.4 jit_solution(1747723572038536245)
XLA Ops:
  6.5 3.4 collective-permute-start
  9.9 7.0 %collective-permute-done = bf16[8,256,128]{2,1,0:T(8,128)(2,1)S(1)} collective-permute-done((bf16[8,256,128]{2,1,0:T(8,128)(2,1)}, bf16[8,256,128]{2,1,0:T(8,128)(2,1)S(1)}, u32[]{:S(2)}, u32[]{:S(2)}) %collective-permute-start) | collective-permute-done | bytes 524320 | tf_op jit(solution)/shard_map/ppermute | solution.py:32
  16.9 2.7 collective-permute-start.1
  19.6 6.7 %collective-permute-done.1 = bf16[8,256,128]{2,1,0:T(8,128)(2,1)S(1)} collective-permute-done((bf16[8,256,128]{2,1,0:T(8,128)(2,1)S(1)}, bf16[8,256,128]{2,1,0:T(8,128)(2,1)S(1)}, u32[]{:S(2)}, u32[]{:S(2)}) %collective-permute-start.1) | collective-permute-done | bytes 524320 | tf_op jit(solution)/shard_map/ppermute | solution.py:32
  26.3 2.8 collective-permute-start.2
  29.1 6.7 %collective-permute-done.2 = bf16[8,256,128]{2,1,0:T(8,128)(2,1)S(1)} collective-permute-done((bf16[8,256,128]{2,1,0:T(8,128)(2,1)S(1)}, bf16[8,256,128]{2,1,0:T(8,128)(2,1)S(1)}, u32[]{:S(2)}, u32[]{:S(2)}) %collective-permute-start.2) | collective-permute-done | bytes 524320 | tf_op jit(solution)/shard_map/ppermute | solution.py:32
  35.8 2.8 collective-permute-start.3
  38.6 1.4 fusion.42
  40.0 5.3 %collective-permute-done.3 = bf16[8,256,128]{2,1,0:T(8,128)(2,1)S(1)} collective-permute-done((bf16[8,256,128]{2,1,0:T(8,128)(2,1)S(1)}, bf16[8,256,128]{2,1,0:T(8,128)(2,1)S(1)}, u32[]{:S(2)}, u32[]{:S(2)}) %collective-permute-start.3) | collective-permute-done | bytes 524320 | tf_op jit(solution)/shard_map/ppermute | solution.py:32
  45.3 2.8 collective-permute-start.4
  48.9 6.0 %collective-permute-done.4 = bf16[8,256,128]{2,1,0:T(8,128)(2,1)S(1)} collective-permute-done((bf16[8,256,128]{2,1,0:T(8,128)(2,1)S(1)}, bf16[8,256,128]{2,1,0:T(8,128)(2,1)S(1)}, u32[]{:S(2)}, u32[]{:S(2)}) %collective-permute-start.4) | collective-permute-done | bytes 524320 | tf_op jit(solution)/shard_map/ppermute | solution.py:32
  54.8 2.8 collective-permute-start.5
  58.4 6.0 %collective-permute-done.5 = bf16[8,256,128]{2,1,0:T(8,128)(2,1)S(1)} collective-permute-done((bf16[8,256,128]{2,1,0:T(8,128)(2,1)S(1)}, bf16[8,256,128]{2,1,0:T(8,128)(2,1)S(1)}, u32[]{:S(2)}, u32[]{:S(2)}) %collective-permute-start.5) | collective-permute-done | bytes 524320 | tf_op jit(solution)/shard_map/ppermute | solution.py:32
  64.3 2.8 collective-permute-start.6
  67.9 6.0 %collective-permute-done.6 = bf16[8,256,128]{2,1,0:T(8,128)(2,1)S(1)} collective-permute-done((bf16[8,256,128]{2,1,0:T(8,128)(2,1)S(1)}, bf16[8,256,128]{2,1,0:T(8,128)(2,1)S(1)}, u32[]{:S(2)}, u32[]{:S(2)}) %collective-permute-start.6) | collective-permute-done | bytes 524320 | tf_op jit(solution)/shard_map/ppermute | solution.py:32
  73.8 5.2 fusion.28
  79.1 0.6 copy-done.1
  79.8 52.2 %reduce-scatter.3.cloned.1.call-done = f32[8,16,1024]{2,1,0:T(8,128)} async-done(((f32[8,128,1024]{2,1,0:T(8,128)}), f32[8,16,1024]{2,1,0:T(8,128)}) %reduce-scatter.3.cloned.1.call-update) | async-done | bytes 524304 | tf_op jit(solution)/shard_map/reduce_scatter | solution.py:45
  132.0 1.7 fusion.65
  133.6 0.8 divide_convert_fusion
  134.5 27.9 %all-gather.6.cloned.1.call-done = bf16[8,128,1024]{2,1,0:T(8,128)(2,1)} async-done(((bf16[8,16,1024]{2,1,0:T(8,128)(2,1)}), bf16[8,128,1024]{2,1,0:T(8,128)(2,1)}) %all-gather.6.cloned.1.call-update) | async-done | bytes 2097168 | tf_op jit(solution)/shard_map/all_gather | solution.py:47
  162.4 5.1 fusion.29
  168.2 0.5 all-gather.12.cloned.1.call-update
  169.6 35.5 %all-gather.8.cloned.1.call-done = bf16[8,2048,128]{1,2,0:T(8,128)(2,1)} async-done(((bf16[8,256,128]{1,2,0:T(8,128)(2,1)}), bf16[8,2048,128]{1,2,0:T(8,128)(2,1)}) %all-gather.8.cloned.1.call-update) | async-done | bytes 4194320 | tf_op jit(solution)/shard_map/all_gather | solution.py:51
  205.1 3.1 fusion.1
  208.2 79.1 %all-gather.10.cloned.1.call-done = bf16[2048,1024]{1,0:T(8,128)(2,1)} async-done(((bf16[512,1024]{1,0:T(8,128)(2,1)}), bf16[2048,1024]{1,0:T(8,128)(2,1)}) %all-gather.10.cloned.1.call-update) | async-done | bytes 4194320 | tf_op jit(solution)/shard_map/all_gather | solution.py:60
  287.3 9.9 %fusion.8 = f32[8,128,1024]{2,1,0:T(8,128)} fusion(bf16[2048,1024]{1,0:T(8,128)(2,1)} %all-gather.10.cloned.1.call-done, bf16[8,2048,128]{1,2,0:T(8,128)(2,1)} %all-gather.8.cloned.1.call-done, f32[2048]{0:T(1024)S(1)} %copy-done.2, f32[8,128]{1,0:T(8,128)S(1)} %add_rsqrt_fusion), kind=kOutput, calls=%fused_computation.10 | convolution fusion | flops 4303355904 | bytes 12595200 | tf_op jit(solution)/shard_map/ukc,kf->ucf/dot_general | solution.py:57
  297.2 70.7 %all-gather.12.cloned.1.call-done = bf16[2048,1024]{1,0:T(8,128)(2,1)} async-done(((bf16[512,1024]{1,0:T(8,128)(2,1)}), bf16[2048,1024]{1,0:T(8,128)(2,1)}) %all-gather.12.cloned.1.call-update) | async-done | bytes 4194320 | tf_op jit(solution)/shard_map/all_gather | solution.py:66
  368.0 80.7 %all-gather.14.cloned.1.call-done = bf16[1024,2048]{1,0:T(8,128)(2,1)} async-done(((bf16[1024,512]{1,0:T(8,128)(2,1)}), bf16[1024,2048]{1,0:T(8,128)(2,1)}) %all-gather.14.cloned.1.call-update) | async-done | bytes 4194320 | tf_op jit(solution)/shard_map/all_gather | solution.py:70
  448.6 15.2 %convert_bitcast_fusion = bf16[2048,8,128]{0,2,1:T(8,128)(2,1)} fusion(bf16[1024,2048]{1,0:T(8,128)(2,1)} %all-gather.14.cloned.1.call-done, f32[8,128,1024]{2,1,0:T(8,128)} %fusion.8, bf16[2048,1024]{1,0:T(8,128)(2,1)} %all-gather.12.cloned.1.call-done, bf16[8,2048,128]{1,2,0:T(8,128)(2,1)} %all-gather.8.cloned.1.call-done, f32[2048]{0:T(1024)S(1)} %copy-done.2, ...), kind=kOutput, calls=%fused_computation.12 | convolution fusion | flops 8606711808 | bytes 20983808 | tf_op jit(solution)/shard_map/ucf,fk->kuc/dot_general | solution.py:72
  463.9 49.7 %reduce-scatter.5.cloned.1.call-done = bf16[256,8,128]{0,2,1:T(8,128)(2,1)} async-done(((bf16[2048,8,128]{0,2,1:T(8,128)(2,1)}), bf16[256,8,128]{0,2,1:T(8,128)(2,1)}) %reduce-scatter.5.cloned.1.call-update) | async-done | bytes 524304 | tf_op jit(solution)/shard_map/reduce_scatter | solution.py:71
  513.5 2.0 copy.9
  (26 shorter events, 3.7 us)
Async XLA Ops:
  6.5 32.1 %copy-start = (bf16[256,2048]{1,0:T(8,128)(2,1)S(1)}, bf16[256,2048]{1,0:T(8,128)(2,1)}, u32[]{:S(2)}) copy-start(bf16[256,2048]{1,0:T(8,128)(2,1)} %param.11) | copy-start | bytes 3145732
  6.5 125.4 %reduce-scatter.3.cloned.1.call-start = ((), (), s32[]{:S(2)}) async-start(), calls=%async_computation.2 | async-start | bytes 4718592 | tf_op jit(solution)/shard_map/reduce_scatter | solution.py:45
  6.5 10.4 %collective-permute-start = (bf16[8,256,128]{2,1,0:T(8,128)(2,1)}, bf16[8,256,128]{2,1,0:T(8,128)(2,1)S(1)}, u32[]{:S(2)}, u32[]{:S(2)}) collective-permute-start(bf16[8,256,128]{2,1,0:T(8,128)(2,1)} %param.9), channel_id=1, source_target_pairs={{0,7},{1,0},{2,1},{3,2},{4,3},{5,4},{6,5},{7,6},{8,15},{9,8},{10,9... | collective-permute-start | bytes 1572872 | tf_op jit(solution)/shard_map/ppermute | solution.py:32
  16.9 9.4 %collective-permute-start.1 = (bf16[8,256,128]{2,1,0:T(8,128)(2,1)S(1)}, bf16[8,256,128]{2,1,0:T(8,128)(2,1)S(1)}, u32[]{:S(2)}, u32[]{:S(2)}) collective-permute-start(bf16[8,256,128]{2,1,0:T(8,128)(2,1)S(1)} %collective-permute-done), channel_id=1, source_target_pairs={{0,7},{1,0},{2,1},{3,2},{4,3},{5,4},{6,5},{7,6},{8,15},{9,8},{10,9... | collective-permute-start | bytes 1572872 | tf_op jit(solution)/shard_map/ppermute | solution.py:32
  26.3 9.5 %collective-permute-start.2 = (bf16[8,256,128]{2,1,0:T(8,128)(2,1)S(1)}, bf16[8,256,128]{2,1,0:T(8,128)(2,1)S(1)}, u32[]{:S(2)}, u32[]{:S(2)}) collective-permute-start(bf16[8,256,128]{2,1,0:T(8,128)(2,1)S(1)} %collective-permute-done.1), channel_id=1, source_target_pairs={{0,7},{1,0},{2,1},{3,2},{4,3},{5,4},{6,5},{7,6},{8,15},{9,8},{10,9... | collective-permute-start | bytes 1572872 | tf_op jit(solution)/shard_map/ppermute | solution.py:32
  35.8 9.5 %collective-permute-start.3 = (bf16[8,256,128]{2,1,0:T(8,128)(2,1)S(1)}, bf16[8,256,128]{2,1,0:T(8,128)(2,1)S(1)}, u32[]{:S(2)}, u32[]{:S(2)}) collective-permute-start(bf16[8,256,128]{2,1,0:T(8,128)(2,1)S(1)} %collective-permute-done.2), channel_id=1, source_target_pairs={{0,7},{1,0},{2,1},{3,2},{4,3},{5,4},{6,5},{7,6},{8,15},{9,8},{10,9... | collective-permute-start | bytes 1572872 | tf_op jit(solution)/shard_map/ppermute | solution.py:32
  45.3 9.5 %collective-permute-start.4 = (bf16[8,256,128]{2,1,0:T(8,128)(2,1)S(1)}, bf16[8,256,128]{2,1,0:T(8,128)(2,1)S(1)}, u32[]{:S(2)}, u32[]{:S(2)}) collective-permute-start(bf16[8,256,128]{2,1,0:T(8,128)(2,1)S(1)} %collective-permute-done.3), channel_id=1, source_target_pairs={{0,7},{1,0},{2,1},{3,2},{4,3},{5,4},{6,5},{7,6},{8,15},{9,8},{10,9... | collective-permute-start | bytes 1572872 | tf_op jit(solution)/shard_map/ppermute | solution.py:32
  54.8 9.5 %collective-permute-start.5 = (bf16[8,256,128]{2,1,0:T(8,128)(2,1)S(1)}, bf16[8,256,128]{2,1,0:T(8,128)(2,1)S(1)}, u32[]{:S(2)}, u32[]{:S(2)}) collective-permute-start(bf16[8,256,128]{2,1,0:T(8,128)(2,1)S(1)} %collective-permute-done.4), channel_id=1, source_target_pairs={{0,7},{1,0},{2,1},{3,2},{4,3},{5,4},{6,5},{7,6},{8,15},{9,8},{10,9... | collective-permute-start | bytes 1572872 | tf_op jit(solution)/shard_map/ppermute | solution.py:32
  64.3 9.5 %collective-permute-start.6 = (bf16[8,256,128]{2,1,0:T(8,128)(2,1)S(1)}, bf16[8,256,128]{2,1,0:T(8,128)(2,1)S(1)}, u32[]{:S(2)}, u32[]{:S(2)}) collective-permute-start(bf16[8,256,128]{2,1,0:T(8,128)(2,1)S(1)} %collective-permute-done.5), channel_id=1, source_target_pairs={{0,7},{1,0},{2,1},{3,2},{4,3},{5,4},{6,5},{7,6},{8,15},{9,8},{10,9... | collective-permute-start | bytes 1572872 | tf_op jit(solution)/shard_map/ppermute | solution.py:32
  79.0 0.7 copy-start.1
  79.0 83.4 %all-gather.6.cloned.1.call-start = ((), (), s32[]{:S(2)}) async-start(), calls=%async_computation.3 | async-start | bytes 2359296 | tf_op jit(solution)/shard_map/all_gather | solution.py:47
  134.5 70.6 %all-gather.8.cloned.1.call-start = ((), (), s32[]{:S(2)}) async-start(), calls=%async_computation.4 | async-start | bytes 4718592 | tf_op jit(solution)/shard_map/all_gather | solution.py:51
  167.6 119.7 %copy-start.2 = (f32[2048]{0:T(1024)S(1)}, f32[2048]{0:T(1024)}, u32[]{:S(2)}) copy-start(f32[2048]{0:T(1024)} %param.12) | copy-start | bytes 24580
  167.6 119.7 %all-gather.10.cloned.1.call-start = ((), (), s32[]{:S(2)}) async-start(), calls=%async_computation.5 | async-start | bytes 5242880 | tf_op jit(solution)/shard_map/all_gather | solution.py:60
  168.2 199.8 %all-gather.12.cloned.1.call-start = ((), (), s32[]{:S(2)}) async-start(), calls=%async_computation.6 | async-start | bytes 5242880 | tf_op jit(solution)/shard_map/all_gather | solution.py:66
  168.8 279.9 %all-gather.14.cloned.1.call-start = ((), (), s32[]{:S(2)}) async-start(), calls=%async_computation.7 | async-start | bytes 5242880 | tf_op jit(solution)/shard_map/all_gather | solution.py:70
  169.3 344.2 %reduce-scatter.5.cloned.1.call-start = ((), (), s32[]{:S(2)}) async-start(), calls=%async_computation.8 | async-start | bytes 4718592 | tf_op jit(solution)/shard_map/reduce_scatter | solution.py:71
Sparse Core Ops, SparseCore 0:
  79.2 52.7 reduce-scatter.2
  134.6 27.7 all-gather.5
  167.7 37.3 all-gather.7
  206.5 80.7 all-gather.9
  288.7 79.2 all-gather.11
  369.4 79.2 all-gather.13
  464.0 49.5 reduce-scatter.4
